TPU v7x, 32 devices: a whole 2x2x4 slice. The times are simulated.
32 devices in a mesh: row: 4 (over x, core), col: 8 (over z, y).
Axes of the slice: x: 2, y: 2, z: 4, core: 2. Of those that a mesh axis runs over, the one named last changes fastest.
Arguments:
- front_panels: float32 [16, 4, 256, 8, 8, 256], P(None, 'row', 'col'), as said below
- child_update_tiles: float32 [4, 8, 8, 256, 256], P('row', 'col'), may hold values from -2 to 2
- child_rows: int32 [4, 8, 8], P('row', 'col'), may hold values from 0 to 63, as said below
- child_cols: int32 [4, 8, 8], P('row', 'col'), may hold values from 0 to 7
- child_counts: int32 [4, 8], P('row', 'col'), may hold values from 4 to 8, as said below
- row_maps: int32 [4, 8, 8, 256], P('row', 'col'), may hold values from 0 to 255, each once within a row
- col_maps: int32 [4, 8, 8, 256], P('row', 'col'), may hold values from 0 to 255, each once within a row
Outputs:
- factored_front: float32 [16, 4, 256, 8, 8, 256], P(None, 'row', None, None, 'col')
Inputs may be any that keep to these rules, and one draw needn't show every extreme that they name: child_rows[r, c, k] modulo 4 names one of four owner rows; among the live slots of one device at most 2 name the same owner row, and some device sends exactly 2 to some owner; every slot's target tile column is at most its target tile row. `child_counts`: every device of col index 0 has all slots live. `front_panels`: the diagonal of the front dominates its first tile, so that tile stays positive definite after the children are added.
All inputs are finite; a program needn't handle non-finite values.
Results may differ from a plain program's by a relative error of at most 0.0003.
Values sent between devices are 32-bit elements; how exact they have to be, the bound alone decides.
No kernel may reach another device: no remote copies, remote signals or barrier semaphores. Data moves between devices by JAX's collectives and lax.ppermute only.
A program may use at most 320 MiB of HBM per device.

v0:
```python
import jax
import jax.numpy as jnp
from jax import lax
from jax.sharding import PartitionSpec as P


def broadcast(value, axis, source):
    kept = jnp.where(lax.axis_index(axis) == source, value, 0).astype(value.dtype)
    return lax.psum(kept, axis)


def slot_positions(owners, is_live):
    slot_entries = owners.shape[-1]
    earlier = lax.broadcasted_iota(
        jnp.int32, (slot_entries, slot_entries), 0
    ) < lax.broadcasted_iota(jnp.int32, (slot_entries, slot_entries), 1)
    same_owner = (owners[..., :, None] == owners[..., None, :]) & is_live[..., :, None] & earlier
    return jnp.sum(same_owner.astype(jnp.int32), axis=-2)


def on_device(
    front_panels, child_update_tiles, child_rows, child_cols, child_counts, row_maps, col_maps
):
    largest_index = lax.Precision.HIGHEST
    row_size = lax.axis_size("row")
    col_size = lax.axis_size("col")
    my_row = lax.axis_index("row")
    my_col = lax.axis_index("col")
    front_width = front_panels.shape[-1]
    blocks = lax.all_to_all(front_panels, "col", split_axis=4, concat_axis=2, tiled=True)
    row_tiles = blocks.shape[0]
    col_tiles = blocks.shape[3]
    blocks = blocks.reshape(row_tiles, front_width, col_tiles, front_width)
    slot_entries = child_update_tiles.shape[2]
    capacity = slot_entries // 4
    labels = lax.broadcasted_iota(jnp.int32, (1, 1, front_width), 2)
    row_indicator = (row_maps.reshape(slot_entries, front_width)[:, :, None] == labels).astype(
        jnp.float32
    )
    column_indicator = (col_maps.reshape(slot_entries, front_width)[:, :, None] == labels).astype(
        jnp.float32
    )
    shifted_tiles = jnp.einsum(
        "gml,gmq->glq",
        row_indicator,
        child_update_tiles.reshape(slot_entries, front_width, front_width),
        precision=largest_index,
    )
    shifted_tiles = jnp.einsum(
        "afb,abx->afx", shifted_tiles, column_indicator, precision=largest_index
    )
    slot_ids = lax.broadcasted_iota(jnp.int32, (slot_entries,), 0)
    is_live = slot_ids < child_counts.reshape(())
    owners = child_rows.reshape(slot_entries) % row_size
    positions = slot_positions(owners, is_live)
    dest_ids = lax.broadcasted_iota(jnp.int32, (row_size, capacity, slot_entries), 0)
    place_ids = lax.broadcasted_iota(jnp.int32, (row_size, capacity, slot_entries), 1)
    selector = (
        (owners[None, None, :] == dest_ids)
        & (positions[None, None, :] == place_ids)
        & is_live[None, None, :]
    ).astype(jnp.float32)
    outgoing = jnp.einsum(
        "opk,kx->opx",
        selector,
        shifted_tiles.reshape(slot_entries, front_width * front_width),
        precision=largest_index,
    )
    incoming = lax.all_to_all(outgoing, "row", split_axis=0, concat_axis=0, tiled=True)
    all_rows, all_cols, all_counts = (
        lax.all_gather(child_rows, "row", axis=0, tiled=True),
        lax.all_gather(child_cols, "row", axis=0, tiled=True),
        lax.all_gather(child_counts, "row", axis=0, tiled=True),
    )
    source_rows = all_rows.reshape(row_size, slot_entries)
    source_cols = all_cols.reshape(row_size, slot_entries)
    source_live = slot_ids[None, :] < all_counts.reshape(row_size)[:, None]
    source_owner = source_rows % row_size
    source_pos = slot_positions(source_owner, source_live)
    mine = (source_live & (source_owner == my_row)).astype(jnp.float32)
    depth_onehot = (
        (source_rows // row_size)[:, :, None]
        == lax.broadcasted_iota(jnp.int32, (1, 1, row_tiles), 2)
    ).astype(jnp.float32) * mine[:, :, None]
    across_onehot = (
        source_cols[:, :, None] == lax.broadcasted_iota(jnp.int32, (1, 1, col_tiles), 2)
    ).astype(jnp.float32)
    place_onehot = (
        source_pos[:, :, None] == lax.broadcasted_iota(jnp.int32, (1, 1, capacity), 2)
    ).astype(jnp.float32)
    landing = jnp.einsum(
        "ska,skb,skp->absp", depth_onehot, across_onehot, place_onehot, precision=largest_index
    )
    incoming = incoming.reshape(row_size, capacity, front_width, front_width)
    blocks = blocks + jnp.einsum("absp,spxy->axby", landing, incoming, precision=largest_index)
    tile_i = lax.broadcasted_iota(jnp.int32, (row_tiles, 1, col_tiles, 1), 0) * row_size + my_row
    tile_j = lax.broadcasted_iota(jnp.int32, (row_tiles, 1, col_tiles, 1), 2) * col_size + my_col
    flipped = jnp.einsum("axby->aybx", blocks)
    blocks = jnp.where(tile_i == tile_j, 0.5 * (blocks + flipped), blocks)
    identity = jnp.eye(front_width, dtype=jnp.float32)
    corner = blocks[0, :, 0, :]
    at_root = (my_row == 0) & (my_col == 0)
    factor = jnp.linalg.cholesky(jnp.where(at_root, corner, identity))
    factor = broadcast(factor, "row", 0)
    column = blocks[:, :, 0, :].reshape(row_tiles * front_width, front_width)
    solved = jax.scipy.linalg.solve_triangular(factor, column.T, lower=True).T.reshape(
        row_tiles, front_width, front_width
    )
    tile_index = lax.broadcasted_iota(jnp.int32, (row_tiles, 1, 1), 0) * row_size + my_row
    kept = jnp.where(tile_index == 0, factor[None, :, :], solved)
    below = jnp.where(tile_index == 0, 0.0, solved)
    row_panel = broadcast(below, "col", 0)
    group = col_size // row_size
    whole = lax.all_gather(row_panel, "row", axis=0, tiled=True)
    whole = whole.reshape(row_size, col_tiles, group, front_width, front_width)
    picked = lax.dynamic_index_in_dim(whole, my_col % row_size, 0, keepdims=False)
    col_panel = lax.dynamic_index_in_dim(picked, my_col // row_size, 1, keepdims=False)
    blocks = blocks - jnp.einsum("asx,bqx->asbq", row_panel, col_panel, precision=largest_index)
    first_column = jnp.where(my_col == 0, kept, blocks[:, :, 0, :])
    blocks = blocks.at[:, :, 0, :].set(first_column)
    blocks = jnp.where(tile_i >= tile_j, blocks, 0.0)
    return blocks.reshape(row_tiles, 1, front_width, col_tiles, 1, front_width)


def solution(mesh):
    return jax.shard_map(
        on_device,
        mesh=mesh,
        in_specs=(
            P(None, "row", "col", None, None, None),
            P("row", "col", None, None, None),
            P("row", "col", None),
            P("row", "col", None),
            P("row", "col"),
            P("row", "col", None, None),
            P("row", "col", None, None),
        ),
        out_specs=P(None, "row", None, None, "col", None),
        check_vma=False,
    )
```

profile of v0, /device:TPU:0, one launch (start us, length us, event | category | flops | bytes accessed | tf_op | source)
XLA Modules:
  0.0 1470.2 jit_solution(9605571834959242759)
XLA Ops:
  6.5 0.8 and_select_fusion.1
  8.1 2.2 fusion.8
  10.3 2.6 fusion.11
  13.0 2.0 reshape.354
  15.7 4.1 fusion.33
  19.8 4.2 all-to-all-start.1
  24.0 30.6 %copy.67 = f32[16,1,32,8,8,256]{5,3,2,0,1,4:T(8,128)} copy(f32[16,1,32,8,8,256]{5,4,3,2,1,0:T(8,128)} %param.9) | data formatting | bytes 67108864 | tf_op args[0]
  54.6 1.3 copy-done.4
  55.9 7.1 all-to-all-start
  64.2 5.8 all-reduce.1
  70.0 5.0 all_gather.14
  75.0 5.2 all_gather.17
  81.3 3.5 reshape.323
  84.8 30.9 %convolution_bitcast_fusion = f32[256,256,16,8]{1,2,3,0:T(8,128)} fusion(f32[4,2,256,256,1]{3,2,1,0,4:T(8,128)S(1)} %bitcast.110, f32[16,8,4,2]{0,1,3,2:T(8,128)S(1)} %convolution_bitcast_fusion.1), kind=kOutput, calls=%fused_computation.8 | convolution fusion | flops 805306368 | bytes 35655680 | tf_op jit(solution)/shard_map/absp,spxy->axby/dot_general | solution.py:95
  115.7 34.4 %copy.72 = f32[256,256,16,8]{0,1,3,2:T(8,128)} copy(f32[256,256,16,8]{1,2,3,0:T(8,128)} %convolution_bitcast_fusion) | data formatting | bytes 67108864 | tf_op jit(solution)/shard_map/absp,spxy->axby/dot_general | solution.py:95
  150.2 637.7 %all-to-all-done = f32[16,1,32,8,8,256]{5,3,2,0,1,4:T(8,128)} async-done(((f32[16,1,32,8,8,256]{5,3,2,0,1,4:T(8,128)}), f32[16,1,32,8,8,256]{5,3,2,0,1,4:T(8,128)}, u32[]{:S(2)}, u32[]{:S(2)}) %all-to-all-start) | async-done | bytes 33554464 | tf_op jit(solution)/shard_map/all_to_all | solution.py:30
  787.9 22.9 %copy.68 = f32[16,1,32,8,8,256]{5,3,2,4,0,1:T(8,128)} copy(f32[16,1,32,8,8,256]{5,3,2,0,1,4:T(8,128)} %all-to-all-done) | data formatting | bytes 67108864 | tf_op jit(solution)/shard_map/all_to_all | solution.py:30
  810.7 35.0 %copy.73 = f32[16,256,8,256]{1,3,2,0:T(8,128)} copy(f32[16,256,8,256]{3,2,1,0:T(8,128)} %bitcast.104) | data formatting | bytes 67108864 | tf_op jit(solution)/shard_map/reshape | solution.py:33
  845.7 33.5 %bitcast_add_fusion.1 = f32[16,256,8,256]{1,3,2,0:T(8,128)} fusion(f32[16,256,8,256]{1,3,2,0:T(8,128)} %copy.73, f32[256,256,16,8]{0,1,3,2:T(8,128)} %copy.72), kind=kLoop, calls=%fused_computation.5 | loop fusion | flops 8388608 | bytes 100663296 | tf_op jit(solution)/shard_map/add | solution.py:95
  879.2 31.9 %copy.74 = f32[16,256,8,256]{3,1,2,0:T(8,128)} copy(f32[16,256,8,256]{1,3,2,0:T(8,128)} %bitcast_add_fusion.1) | data formatting | bytes 67108864 | tf_op jit(solution)/shard_map/add | solution.py:95
  911.2 33.6 %fusion.1 = f32[16,256,8,256]{1,3,2,0:T(8,128)} fusion(f32[16,256,8,256]{1,3,2,0:T(8,128)} %bitcast_add_fusion.1, f32[16,256,8,256]{3,1,2,0:T(8,128)} %copy.74, pred[16,8]{1,0:T(8,128)(4,1)S(1)} %get-tuple-element.42), kind=kLoop, calls=%fused_computation.4 | loop fusion | flops 25165824 | bytes 100663424 | tf_op jit(solution)/shard_map/jit(_where)/select_n | solution.py:99
  944.8 1.0 fusion.14
  945.9 1.0 fusion.15
  947.0 11.7 cholesky.50
  958.7 9.8 custom-call.15
  969.0 11.7 cholesky.105
  983.6 4.5 slice.96
  988.1 5.8 copy.76
  993.9 5.7 copy.77
  999.6 14.6 all-reduce.5.cloned.1.call-done
  1014.1 1.0 fusion.16
  1015.2 3.9 while.2
  1015.8 1.3 bitcast_dynamic-update-slice_fusion.3
  1017.7 1.3 bitcast_dynamic-update-slice_fusion.3
  1019.0 19.7 %custom-call.16 = f32[2,128,128]{1,2,0:T(8,128)S(1)} custom-call(f32[2,128,128]{2,1,0:T(8,128)S(1)} %get-tuple-element.24), custom_call_target="InvertDiagBlocksLowerTriangular" | custom-call | tf_op jit(solution)/shard_map/jit(_solve_triangular)/triangular_solve | solution.py:106
  1038.7 3.6 fusion.4
  1042.4 1.9 convolution_subtract_fusion.1
  1044.3 1.9 fusion.18
  1046.3 2.4 maximum_bitcast_fusion
  1048.6 5.6 copy.94
  1054.2 4.7 select_select_fusion
  1059.0 156.4 %all-reduce.7.cloned.1.call-done = f32[16,256,256]{2,1,0:T(8,128)} async-done(((f32[16,256,256]{2,1,0:T(8,128)}), f32[16,256,256]{2,1,0:T(8,128)}) %all-reduce.7.cloned.1.call-update) | async-done | bytes 4194320 | tf_op jit(solution)/shard_map/psum | solution.py:9
  1215.5 5.6 copy.83
  1221.2 100.9 %all-gather.2.cloned.1.call-done = f32[64,256,256]{2,1,0:T(8,128)} async-done(((f32[16,256,256]{2,1,0:T(8,128)}), f32[64,256,256]{2,1,0:T(8,128)}) %all-gather.2.cloned.1.call-update) | async-done | bytes 16777232 | tf_op jit(solution)/shard_map/all_gather | solution.py:114
  1322.0 35.3 %convolution_subtract_fusion = f32[16,256,8,256]{1,3,2,0:T(8,128)} fusion(f32[16,256,8,256]{1,3,2,0:T(8,128)} %fusion.1, f32[16,256,256]{2,1,0:T(8,128)} %all-reduce.7.cloned.1.call-done, f32[4,8,2,256,256]{4,3,2,1,0:T(8,128)} %bitcast.111, s32[]{:T(128)S(6)} %select_n.139, s32[]{:T(128)S(6)} %select_n.142), kind=kOutput, calls=%fused_computation.7 | convolution fusion | flops 25778192384 | bytes 73400328 | tf_op jit(solution)/shard_map/asx,bqx->asbq/dot_general | solution.py:118
  1357.3 4.8 fusion.2
  1362.2 22.9 %select_bitcast_fusion = f32[16,1,256,8,1,256]{2,5,3,0,4,1:T(8,128)} fusion(f32[16,256,8,256]{1,3,2,0:T(8,128)} %fusion.2, pred[16,8]{1,0:T(8,128)(4,1)S(1)} %copy-done.6), kind=kLoop, calls=%fused_computation.6 | loop fusion | flops 8388608 | bytes 67108992 | tf_op jit(solution)/shard_map/reshape | solution.py:122
  1385.1 78.3 %copy.84 = f32[16,1,256,8,1,256]{5,4,3,2,1,0:T(1,128)} copy(f32[16,1,256,8,1,256]{2,5,3,0,4,1:T(8,128)} %select_bitcast_fusion) | data formatting | bytes 67108864 | tf_op jit(solution)/shard_map/reshape | solution.py:122
  (64 shorter events, 6.9 us)
Async XLA Ops:
  6.5 1.6 copy-start
  6.5 3.8 copy-start.7
  19.8 34.8 %all-to-all-start.1 = ((f32[4,2,65536]{2,1,0:T(2,128)}), f32[4,2,65536]{2,1,0:T(2,128)S(1)}, u32[]{:S(2)}, u32[]{:S(2)}) async-start(f32[4,2,65536]{2,1,0:T(2,128)} %fusion.33), calls=%async_computation.1 | async-start | bytes 4194304 | tf_op jit(solution)/shard_map/all_to_all | solution.py:69
  54.6 8.5 copy-start.10
  54.6 15.4 %copy-start.8 = (s32[1,1,8]{2,1,0:T(1,128)S(1)}, s32[1,1,8]{2,1,0:T(1,128)}, u32[]{:S(2)}) copy-start(s32[1,1,8]{2,1,0:T(1,128)} %param.11) | copy-start | bytes 100
  54.6 20.5 %copy-start.9 = (s32[1,1,8]{2,1,0:T(1,128)S(1)}, s32[1,1,8]{2,1,0:T(1,128)}, u32[]{:S(2)}) copy-start(s32[1,1,8]{2,1,0:T(1,128)} %param.12) | copy-start | bytes 100
  54.6 1.3 copy-start.4
  55.9 731.9 %all-to-all-start = ((f32[16,1,32,8,8,256]{5,3,2,0,1,4:T(8,128)}), f32[16,1,32,8,8,256]{5,3,2,0,1,4:T(8,128)}, u32[]{:S(2)}, u32[]{:S(2)}) async-start(f32[16,1,32,8,8,256]{5,3,2,0,1,4:T(8,128)} %copy.67), calls=%async_computation | async-start | bytes 67108864 | tf_op jit(solution)/shard_map/all_to_all | solution.py:30
  63.0 951.1 %all-reduce.5.cloned.1.call-start = ((), (), s32[]{:S(2)}) async-start(), calls=%async_computation.2 | async-start | bytes 524288 | tf_op jit(solution)/shard_map/psum | solution.py:9
  983.5 231.9 %all-reduce.7.cloned.1.call-start = ((), (), s32[]{:S(2)}) async-start(), calls=%async_computation.3 | async-start | bytes 8388608 | tf_op jit(solution)/shard_map/psum | solution.py:9
  1038.7 3.7 copy-start.3
  1059.0 263.1 %all-gather.2.cloned.1.call-start = ((), (), s32[]{:S(2)}) async-start(), calls=%async_computation.4 | async-start | bytes 20971520 | tf_op jit(solution)/shard_map/all_gather | solution.py:114
  1215.5 5.6 copy-start.5
  1322.0 35.3 %copy-start.2 = (f32[16,256,1,256]{1,3,2,0:T(8,128)S(1)}, f32[16,256,1,256]{1,3,2,0:T(8,128)}, u32[]{:S(2)}) copy-start(f32[16,256,1,256]{1,3,2,0:T(8,128)} %copy.83) | copy-start | bytes 12582916
  1357.3 4.8 copy-start.6
  1385.1 78.3 %copy-start.1 = (f32[1,1,8,256,256]{4,3,2,1,0:T(8,128)S(1)}, f32[1,1,8,256,256]{4,3,2,1,0:T(8,128)}, u32[]{:S(2)}) copy-start(f32[1,1,8,256,256]{4,3,2,1,0:T(8,128)} %param.10) | copy-start | bytes 6291460
Sparse Core Ops, SparseCore 0:
  983.6 30.4 all-reduce.4
  1059.1 156.2 all-reduce.6
  1217.1 104.9 all-gather.1
where the time goes:
time: 1480 us; the launch traced here: 1470 us
  waiting for transfers between devices  910 us (61%)
  local copies, waits for them, and re-layouts  273 us (18%)
  other arithmetic  162 us (11%)
  matrix products  83.3 us (6%)
  blocking collectives  16 us (1%)
  between operations  15.5 us (1%)
    all_to_all x1, waiting for transfers between devices, on_device(): lax.all_to_all(front_panels, 'col', split_axis=4, concat_axis=2, tiled=True)  638 us
    psum x2, waiting for transfers between devices, broadcast(): return lax.psum(kept, axis)  171 us
    all_gather x1, waiting for transfers between devices, on_device(): whole = lax.all_gather(row_panel, 'row', axis=0, tiled=True)  101 us
    reshape x1, local copies, waits for them, and re-layouts, on_device(): return blocks.reshape(row_tiles, 1, front_width, col_tiles, 1, front_width)  78.3 us
    dot_general x1, matrix products, on_device(): jnp.einsum('asx,bqx->asbq', row_panel, col_panel, precision=largest_index)  35.3 us
    reshape x1, local copies, waits for them, and re-layouts, on_device(): blocks = blocks.reshape(row_tiles, front_width, col_tiles, front_width)  35 us
    dot_general x1, local copies, waits for them, and re-layouts, on_device(): jnp.einsum('absp,spxy->axby', landing, incoming, precision=largest_index)  34.4 us
    another operation x6, other arithmetic, on_device(): factor = jnp.linalg.cholesky(jnp.where(at_root, corner, identity))  34 us
  transfers between devices with their start and end apart: 5, of which 4 were waited for; matrix products, arithmetic and copies ran while one was open for 8% of the time, Pallas kernels for 0%

commit v1 on v0

--- a/solution.py
+++ b/solution.py
@@ -27,7 +27,10 @@
     my_row = lax.axis_index("row")
     my_col = lax.axis_index("col")
     front_width = front_panels.shape[-1]
-    blocks = lax.all_to_all(front_panels, "col", split_axis=4, concat_axis=2, tiled=True)
+    n_dev = lax.axis_size("col")
+    pieces = jnp.stack(jnp.split(front_panels, n_dev, axis=4), axis=0)
+    pieces = lax.all_to_all(pieces, "col", split_axis=0, concat_axis=0)
+    blocks = jnp.concatenate(pieces, axis=2)
     row_tiles = blocks.shape[0]
     col_tiles = blocks.shape[3]
     blocks = blocks.reshape(row_tiles, front_width, col_tiles, front_width)

time: 1480 us -> 1570 us (1.061)
  local copies, waits for them, and re-layouts: 273 us -> 364 us
    split x0 -> x1, local copies, waits for them, and re-layouts: none -> 92.8 us  [on_device(): pieces = jnp.stack(jnp.split(front_panels, n_dev, axis=4), axis=0)]
    another operation x6 -> x8, local copies, waits for them, and re-layouts: 3.82 us -> 41 us  [the longest x1 35 us: on_device(): blocks = blocks.reshape(row_tiles, front_width, col_tiles, front_width)]
    reshape x1 -> x0, local copies, waits for them, and re-layouts: 35 us -> none  [on_device(): blocks = blocks.reshape(row_tiles, front_width, col_tiles, front_width)]
    unnamed x26 -> x46, local copies, waits for them, and re-layouts: 33.2 us -> 29.6 us
  transfers between devices with their start and end apart: 5 -> 5, of which waited for: 4 -> 4; matrix products, arithmetic and copies ran while one was open for 8% -> 13% of each run, Pallas kernels for 0% -> 0%
where the time goes in v1:
time: 1570 us; the launch traced here: 1560 us
  waiting for transfers between devices  910 us (58%)
  local copies, waits for them, and re-layouts  364 us (23%)
  other arithmetic  162 us (10%)
  matrix products  83.3 us (5%)
  blocking collectives  15.8 us (1%)
    all_to_all x1, waiting for transfers between devices, on_device(): pieces = lax.all_to_all(pieces, 'col', split_axis=0, concat_axis=0)  638 us
    psum x2, waiting for transfers between devices, broadcast(): return lax.psum(kept, axis)  171 us
    all_gather x1, waiting for transfers between devices, on_device(): whole = lax.all_gather(row_panel, 'row', axis=0, tiled=True)  101 us
    split x1, local copies, waits for them, and re-layouts, on_device(): pieces = jnp.stack(jnp.split(front_panels, n_dev, axis=4), axis=0)  92.8 us
    reshape x1, local copies, waits for them, and re-layouts, on_device(): return blocks.reshape(row_tiles, 1, front_width, col_tiles, 1, front_width)  78.3 us
    dot_general x1, matrix products, on_device(): jnp.einsum('asx,bqx->asbq', row_panel, col_panel, precision=largest_index)  35.3 us
    another operation x1, local copies, waits for them, and re-layouts, on_device(): blocks = blocks.reshape(row_tiles, front_width, col_tiles, front_width)  35 us
    dot_general x1, local copies, waits for them, and re-layouts, on_device(): jnp.einsum('absp,spxy->axby', landing, incoming, precision=largest_index)  34.4 us
  transfers between devices with their start and end apart: 5, of which 4 were waited for; matrix products, arithmetic and copies ran while one was open for 13% of the time, Pallas kernels for 0%

profile of v1, /device:TPU:0, one launch (start us, length us, event | category | flops | bytes accessed | tf_op | source)
XLA Modules:
  0.0 1561.6 jit_solution(3904566239132187786)
XLA Ops:
  8.7 2.2 fusion.16
  10.9 2.6 fusion.19
  13.5 2.0 reshape.353
  15.6 4.0 fusion.41
  19.6 4.2 all-to-all-start.1
  23.8 92.8 %fusion.53 = (f32[16,1,32,8,1,256]{5,4,3,2,1,0:T(1,128)}, f32[16,1,32,8,1,256]{5,4,3,2,1,0:T(1,128)}, f32[16,1,32,8,1,256]{5,4,3,2,1,0:T(1,128)}, f32[16,1,32,8,...) fusion(f32[16,1,32,8,8,256]{5,4,3,2,1,0:T(8,128)} %param.9), kind=kLoop, calls=%fused_computation.126 | loop fusion | bytes 67108864 | tf_op jit(solution)/shard_map/split | solution.py:31
  116.6 4.7 fusion.10
  121.4 2.6 fusion.9
  125.1 2.6 fusion.8
  128.8 2.6 fusion.7
  132.5 2.6 fusion.6
  136.2 2.6 fusion.5
  139.9 2.6 fusion.4
  143.6 2.4 fusion.3
  147.4 7.3 all-to-all-start
  156.0 5.8 all-reduce.1
  161.8 5.0 all_gather.14
  166.8 5.0 all_gather.17
  172.9 3.5 reshape.322
  176.4 30.9 %convolution_bitcast_fusion = f32[256,256,16,8]{1,2,3,0:T(8,128)} fusion(f32[4,2,256,256,1]{3,2,1,0,4:T(8,128)S(1)} %bitcast.140, f32[16,8,4,2]{0,1,3,2:T(8,128)S(1)} %convolution_bitcast_fusion.1), kind=kOutput, calls=%fused_computation.8 | convolution fusion | flops 805306368 | bytes 35655680 | tf_op jit(solution)/shard_map/absp,spxy->axby/dot_general | solution.py:98
  207.3 34.4 %copy.100 = f32[256,256,16,8]{0,1,3,2:T(8,128)} copy(f32[256,256,16,8]{1,2,3,0:T(8,128)} %convolution_bitcast_fusion) | data formatting | bytes 67108864 | tf_op jit(solution)/shard_map/absp,spxy->axby/dot_general | solution.py:98
  241.7 637.7 %all-to-all-done = f32[8,16,1,32,8,1,256]{6,4,3,1,5,2,0:T(8,128)} async-done(((f32[8,16,1,32,8,1,256]{6,4,3,1,5,2,0:T(8,128)}), f32[8,16,1,32,8,1,256]{6,4,3,1,5,2,0:T(8,128)}, u32[]{:S(2)}, u32[]{:S(2)}) %all-to-all-start) | async-done | bytes 33554464 | tf_op jit(solution)/shard_map/all_to_all | solution.py:32
  879.5 22.9 %copy.96 = f32[8,16,1,32,8,1,256]{6,4,3,0,1,5,2:T(8,128)} copy(f32[8,16,1,32,8,1,256]{6,4,3,1,5,2,0:T(8,128)} %all-to-all-done) | data formatting | bytes 67108864 | tf_op jit(solution)/shard_map/all_to_all | solution.py:32
  902.3 35.0 %copy.101 = f32[16,256,8,256]{1,3,2,0:T(8,128)} copy(f32[16,256,8,256]{3,2,1,0:T(8,128)} %bitcast.134) | data formatting | bytes 67108864 | tf_op jit(solution)/shard_map/reshape;reshape | solution.py:36
  937.3 33.5 %bitcast_add_fusion.1 = f32[16,256,8,256]{1,3,2,0:T(8,128)} fusion(f32[16,256,8,256]{1,3,2,0:T(8,128)} %copy.101, f32[256,256,16,8]{0,1,3,2:T(8,128)} %copy.100), kind=kLoop, calls=%fused_computation.5 | loop fusion | flops 8388608 | bytes 100663296 | tf_op jit(solution)/shard_map/add | solution.py:98
  970.9 32.0 %copy.102 = f32[16,256,8,256]{3,1,2,0:T(8,128)} copy(f32[16,256,8,256]{1,3,2,0:T(8,128)} %bitcast_add_fusion.1) | data formatting | bytes 67108864 | tf_op jit(solution)/shard_map/add | solution.py:98
  1002.9 33.6 %fusion.1 = f32[16,256,8,256]{1,3,2,0:T(8,128)} fusion(f32[16,256,8,256]{1,3,2,0:T(8,128)} %bitcast_add_fusion.1, f32[16,256,8,256]{3,1,2,0:T(8,128)} %copy.102, pred[16,8]{1,0:T(8,128)(4,1)S(1)} %get-tuple-element.50), kind=kLoop, calls=%fused_computation.4 | loop fusion | flops 25165824 | bytes 100663424 | tf_op jit(solution)/shard_map/jit(_where)/select_n | solution.py:102
  1038.6 11.7 cholesky.50
  1050.4 9.8 custom-call.15
  1060.7 11.7 cholesky.105
  1075.3 4.5 slice.96
  1079.8 5.8 copy.104
  1085.6 5.7 copy.105
  1091.3 14.5 all-reduce.5.cloned.1.call-done
  1106.8 3.6 while.2
  1110.4 19.7 %custom-call.16 = f32[2,128,128]{1,2,0:T(8,128)S(1)} custom-call(f32[2,128,128]{2,1,0:T(8,128)S(1)} %get-tuple-element.24), custom_call_target="InvertDiagBlocksLowerTriangular" | custom-call | tf_op jit(solution)/shard_map/jit(_solve_triangular)/triangular_solve | solution.py:109
  1130.1 3.6 fusion.12
  1135.7 1.9 fusion.26
  1137.7 2.4 maximum_bitcast_fusion
  1140.0 5.6 copy.122
  1145.7 4.7 select_select_fusion
  1150.4 156.4 %all-reduce.7.cloned.1.call-done = f32[16,256,256]{2,1,0:T(8,128)} async-done(((f32[16,256,256]{2,1,0:T(8,128)}), f32[16,256,256]{2,1,0:T(8,128)}) %all-reduce.7.cloned.1.call-update) | async-done | bytes 4194320 | tf_op jit(solution)/shard_map/psum | solution.py:9
  1306.9 5.6 copy.111
  1312.6 100.9 %all-gather.2.cloned.1.call-done = f32[64,256,256]{2,1,0:T(8,128)} async-done(((f32[16,256,256]{2,1,0:T(8,128)}), f32[64,256,256]{2,1,0:T(8,128)}) %all-gather.2.cloned.1.call-update) | async-done | bytes 16777232 | tf_op jit(solution)/shard_map/all_gather | solution.py:117
  1413.5 35.3 %convolution_subtract_fusion = f32[16,256,8,256]{1,3,2,0:T(8,128)} fusion(f32[16,256,8,256]{1,3,2,0:T(8,128)} %fusion.1, f32[16,256,256]{2,1,0:T(8,128)} %all-reduce.7.cloned.1.call-done, f32[4,8,2,256,256]{4,3,2,1,0:T(8,128)} %bitcast.141, s32[]{:T(128)S(6)} %select_n.139, s32[]{:T(128)S(6)} %select_n.142), kind=kOutput, calls=%fused_computation.7 | convolution fusion | flops 25778192384 | bytes 73400328 | tf_op jit(solution)/shard_map/asx,bqx->asbq/dot_general | solution.py:121
  1448.8 4.8 fusion.2
  1453.6 22.9 %select_bitcast_fusion = f32[16,1,256,8,1,256]{2,5,3,0,4,1:T(8,128)} fusion(f32[16,256,8,256]{1,3,2,0:T(8,128)} %fusion.2, pred[16,8]{1,0:T(8,128)(4,1)S(1)} %copy-done.13), kind=kLoop, calls=%fused_computation.6 | loop fusion | flops 8388608 | bytes 67108992 | tf_op jit(solution)/shard_map/reshape | solution.py:125
  1476.5 78.3 %copy.112 = f32[16,1,256,8,1,256]{5,4,3,2,1,0:T(1,128)} copy(f32[16,1,256,8,1,256]{2,5,3,0,4,1:T(8,128)} %select_bitcast_fusion) | data formatting | bytes 67108864 | tf_op jit(solution)/shard_map/reshape | solution.py:125
  (86 shorter events, 23.0 us)
Async XLA Ops:
  6.5 2.1 copy-start
  6.5 4.4 copy-start.14
  19.6 126.4 %all-to-all-start.1 = ((f32[4,2,65536]{2,1,0:T(2,128)}), f32[4,2,65536]{2,1,0:T(2,128)S(1)}, u32[]{:S(2)}, u32[]{:S(2)}) async-start(f32[4,2,65536]{2,1,0:T(2,128)} %fusion.41), calls=%async_computation.1 | async-start | bytes 4194304 | tf_op jit(solution)/shard_map/all_to_all | solution.py:72
  116.6 4.7 copy-start.9
  121.4 3.7 copy-start.8
  125.1 3.7 copy-start.7
  128.8 3.7 copy-start.5
  132.5 3.7 copy-start.4
  136.2 3.7 copy-start.3
  139.9 3.7 copy-start.2
  146.0 8.7 copy-start.17
  146.0 15.7 %copy-start.15 = (s32[1,1,8]{2,1,0:T(1,128)S(1)}, s32[1,1,8]{2,1,0:T(1,128)}, u32[]{:S(2)}) copy-start(s32[1,1,8]{2,1,0:T(1,128)} %param.11) | copy-start | bytes 100
  146.0 20.8 %copy-start.16 = (s32[1,1,8]{2,1,0:T(1,128)S(1)}, s32[1,1,8]{2,1,0:T(1,128)}, u32[]{:S(2)}) copy-start(s32[1,1,8]{2,1,0:T(1,128)} %param.12) | copy-start | bytes 100
  146.0 1.3 copy-start.11
  147.4 732.1 %all-to-all-start = ((f32[8,16,1,32,8,1,256]{6,4,3,1,5,2,0:T(8,128)}), f32[8,16,1,32,8,1,256]{6,4,3,1,5,2,0:T(8,128)}, u32[]{:S(2)}, u32[]{:S(2)}) async-start(f32[8,16,1,32,8,1,256]{6,4,3,1,5,2,0:T(8,128)} %fusion.3), calls=%async_computation | async-start | bytes 67108864 | tf_op jit(solution)/shard_map/all_to_all | solution.py:32
  154.6 951.2 %all-reduce.5.cloned.1.call-start = ((), (), s32[]{:S(2)}) async-start(), calls=%async_computation.2 | async-start | bytes 524288 | tf_op jit(solution)/shard_map/psum | solution.py:9
  1075.2 231.7 %all-reduce.7.cloned.1.call-start = ((), (), s32[]{:S(2)}) async-start(), calls=%async_computation.3 | async-start | bytes 8388608 | tf_op jit(solution)/shard_map/psum | solution.py:9
  1130.1 3.7 copy-start.10
  1150.4 263.1 %all-gather.2.cloned.1.call-start = ((), (), s32[]{:S(2)}) async-start(), calls=%async_computation.4 | async-start | bytes 20971520 | tf_op jit(solution)/shard_map/all_gather | solution.py:117
  1306.9 5.6 copy-start.12
  1413.5 35.3 %copy-start.6 = (f32[16,256,1,256]{1,3,2,0:T(8,128)S(1)}, f32[16,256,1,256]{1,3,2,0:T(8,128)}, u32[]{:S(2)}) copy-start(f32[16,256,1,256]{1,3,2,0:T(8,128)} %copy.111) | copy-start | bytes 12582916
  1448.8 4.8 copy-start.13
  1476.5 78.3 %copy-start.1 = (f32[1,1,8,256,256]{4,3,2,1,0:T(8,128)S(1)}, f32[1,1,8,256,256]{4,3,2,1,0:T(8,128)}, u32[]{:S(2)}) copy-start(f32[1,1,8,256,256]{4,3,2,1,0:T(8,128)} %param.10) | copy-start | bytes 6291460
Sparse Core Ops, SparseCore 0:
  1075.3 30.4 all-reduce.4
  1150.5 156.2 all-reduce.6
  1308.5 104.9 all-gather.1
